TPU v7x, 32 devices: a whole 2x2x4 slice. The times are simulated.
32 devices in a mesh: wide: 8 (over y, x, core), tp: 4 (over z).
Axes of the slice: x: 2, y: 2, z: 4, core: 2. Of those that a mesh axis runs over, the one named last changes fastest.
Arguments:
- hidden_in: bfloat16 [8, 1024, 1024], P('tp', 'wide'), may hold values from -6 to 6
- lengths: int32 [8], replicated, may hold values from 256 to 1024, as said below
- pre_gain: bfloat16 [1024], P('wide'), may hold values from 0.5 to 1.5
- pre_shift: bfloat16 [1024], P('wide'), may hold values from -1.796875 to 1.796875
- w_query: bfloat16 [1024, 1024], P('wide', 'tp'), may hold values from -0.1875 to 0.1875
- w_key: bfloat16 [1024, 1024], P('wide', 'tp'), may hold values from -0.1875 to 0.1875
- w_value: bfloat16 [1024, 1024], P('wide', 'tp'), may hold values from -0.1875 to 0.1875
- b_query: bfloat16 [16, 64], P('tp', 'wide'), may hold values from -1.796875 to 1.796875
- b_value: bfloat16 [16, 64], P('tp', 'wide'), may hold values from -1.796875 to 1.796875
- w_dense: bfloat16 [1024, 1024], P('tp', 'wide'), may hold values from -0.75 to 0.75
- b_dense: bfloat16 [1024], P('wide'), may hold values from -1.796875 to 1.796875
- mid_gain: bfloat16 [1024], P('wide'), may hold values from 0.5 to 1.5
- mid_shift: bfloat16 [1024], P('wide'), may hold values from -1.796875 to 1.796875
- w_up: bfloat16 [1024, 4096], P('wide', 'tp'), may hold values from -0.1875 to 0.1875
- b_up: bfloat16 [16, 256], P('tp', 'wide'), may hold values from -1.796875 to 1.796875
- w_down: bfloat16 [4096, 1024], P('tp', 'wide'), may hold values from -0.09375 to 0.09375
- b_down: bfloat16 [1024], P('wide'), may hold values from -1.796875 to 1.796875
- cotangent: bfloat16 [8, 1024, 1024], P('tp', 'wide'), may hold values from -6 to 6
Outputs:
- output: bfloat16 [8, 1024, 1024], P('tp', 'wide')
- grad_in: bfloat16 [8, 1024, 1024], P('tp', 'wide')
- grad_pre_gain: float32 [1024], P('wide')
- grad_pre_shift: float32 [1024], P('wide')
- grad_w_query: float32 [1024, 1024], P('wide', 'tp')
- grad_w_key: float32 [1024, 1024], P('wide', 'tp')
- grad_w_value: float32 [1024, 1024], P('wide', 'tp')
- grad_b_query: float32 [16, 64], P('tp', 'wide')
- grad_b_value: float32 [16, 64], P('tp', 'wide')
- grad_w_dense: float32 [1024, 1024], P('tp', 'wide')
- grad_b_dense: float32 [1024], P('wide')
- grad_mid_gain: float32 [1024], P('wide')
- grad_mid_shift: float32 [1024], P('wide')
- grad_w_up: float32 [1024, 4096], P('wide', 'tp')
- grad_b_up: float32 [16, 256], P('tp', 'wide')
- grad_w_down: float32 [4096, 1024], P('tp', 'wide')
- grad_b_down: float32 [1024], P('wide')
Inputs may be any that keep to these rules, and one draw needn't show every extreme that they name: lengths[s] tokens fill the leading positions of slot s; some slot is full and some holds exactly 256 tokens.
All inputs are finite; a program needn't handle non-finite values.
Results may differ from a plain program's by a relative error of at most 0.02.
Values may be sent and summed in bfloat16 or wider, within the bound.
A program may use at most 192 MiB of HBM per device.

v0:
```python
import math
import jax
import jax.numpy as jnp
from jax import lax
from jax.sharding import PartitionSpec as P

HEAD = 64


def norm_rows(values, gain_vec, shift_vec):
    middle = jnp.mean(values, axis=-1, keepdims=True)
    centred = values - middle
    spread = jnp.mean(centred * centred, axis=-1, keepdims=True)
    return centred * lax.rsqrt(spread + 1e-05) * gain_vec + shift_vec


def flatten_rows(tensor):
    return tensor.reshape(-1, tensor.shape[-1])


def row_product(first_op, second_op):
    return jnp.dot(first_op, second_op, preferred_element_type=jnp.float32)


def inner_rows(first_op, second_op):
    return lax.dot_general(
        flatten_rows(first_op),
        flatten_rows(second_op),
        (((0,), (0,)), ((), ())),
        preferred_element_type=jnp.float32,
    )


def times_transposed(first_op, second_op):
    return lax.dot_general(
        first_op,
        second_op,
        (((first_op.ndim - 1,), (1,)), ((), ())),
        preferred_element_type=jnp.float32,
    )


def activate(values):
    return jax.nn.gelu(values, approximate=True)


def masked_scores(query_blk, key_blk, lengths_blk, slopes, distance, causal_mask, key_places):
    raw_scores = (
        jnp.einsum("gihd,gjhd->ghij", query_blk, key_blk, preferred_element_type=jnp.float32)
        * 0.125
    )
    raw_scores = raw_scores - slopes[None, :, None, None] * distance[None, None]
    allowed = causal_mask[None] & (key_places[None, None, :] < lengths_blk[:, None, None])
    return jnp.where(allowed[:, None], raw_scores, -jnp.inf)


def per_device(
    hidden_in,
    lengths,
    pre_gain,
    pre_shift,
    w_query,
    w_key,
    w_value,
    b_query,
    b_value,
    w_dense,
    b_dense,
    mid_gain,
    mid_shift,
    w_up,
    b_up,
    w_down,
    b_down,
    cotangent,
):
    local_slots, block_len, _unused = hidden_in.shape
    heads_dev = b_query.shape[0]
    head_width = heads_dev * HEAD
    slot_total = local_slots * lax.axis_size("tp")
    slot_len = block_len * lax.axis_size("wide")
    wide_at = lax.axis_index("wide")
    tp_at = lax.axis_index("tp")
    vec_part = pre_gain.shape[0]
    (
        gain_one,
        shift_one,
        query_w,
        key_w,
        value_w,
        query_b,
        value_b,
        dense_w,
        dense_b,
        gain_two,
        shift_two,
        up_w,
        up_b,
        down_w,
        down_b,
    ) = (
        lax.all_gather(pre_gain, "wide", axis=0, tiled=True),
        lax.all_gather(pre_shift, "wide", axis=0, tiled=True),
        lax.all_gather(w_query, "wide", axis=0, tiled=True),
        lax.all_gather(w_key, "wide", axis=0, tiled=True),
        lax.all_gather(w_value, "wide", axis=0, tiled=True),
        lax.all_gather(b_query, "wide", axis=1, tiled=True),
        lax.all_gather(b_value, "wide", axis=1, tiled=True),
        lax.all_gather(w_dense, "wide", axis=1, tiled=True),
        lax.all_gather(b_dense, "wide", axis=0, tiled=True),
        lax.all_gather(mid_gain, "wide", axis=0, tiled=True),
        lax.all_gather(mid_shift, "wide", axis=0, tiled=True),
        lax.all_gather(w_up, "wide", axis=0, tiled=True),
        lax.all_gather(b_up, "wide", axis=1, tiled=True),
        lax.all_gather(w_down, "wide", axis=1, tiled=True),
        lax.all_gather(b_down, "wide", axis=0, tiled=True),
    )
    gain_one = gain_one.astype(jnp.float32)
    shift_one = shift_one.astype(jnp.float32)
    gain_two = gain_two.astype(jnp.float32)
    shift_two = shift_two.astype(jnp.float32)
    query_places = wide_at * block_len + jnp.arange(block_len, dtype=jnp.int32)
    key_places = jnp.arange(slot_len, dtype=jnp.int32)
    distance = (query_places[:, None] - key_places[None, :]).astype(jnp.float32)
    causal_mask = key_places[None, :] <= query_places[:, None]
    head_index = tp_at * heads_dev + jnp.arange(heads_dev, dtype=jnp.int32)
    slopes = jnp.exp2(-0.5 * (head_index.astype(jnp.float32) + 1.0))
    own_lengths = lax.dynamic_slice_in_dim(lengths, tp_at * local_slots, local_slots, 0)
    validity = (query_places[None, :] < own_lengths[:, None]).astype(jnp.float32)
    group_size = math.gcd(slot_total, max(1, 512 // block_len))
    group_count = slot_total // group_size
    grouped_lengths = lengths.reshape(group_count, group_size)
    hidden = hidden_in.astype(jnp.float32)

    def query_view(tensor):
        return tensor.reshape(group_count, group_size, block_len, heads_dev, HEAD)

    def pair_view(tensor):
        return tensor.reshape(group_count, group_size, slot_len, 2, heads_dev, HEAD)

    def forward_group(inputs):
        query_blk, pair_blk, lengths_blk = inputs
        masked = masked_scores(
            query_blk, pair_blk[:, :, 0], lengths_blk, slopes, distance, causal_mask, key_places
        )
        highest = jnp.max(masked, axis=-1, keepdims=True)
        totals = highest + jnp.log(jnp.sum(jnp.exp(masked - highest), axis=-1, keepdims=True))
        probabilities = jnp.exp(masked - totals).astype(jnp.bfloat16)
        summed = jnp.einsum(
            "ghij,gjhd->gihd", probabilities, pair_blk[:, :, 1], preferred_element_type=jnp.float32
        )
        return (totals[..., 0], summed)

    def attention_forward(hidden_rows):
        normed_f, norm_back = jax.vjp(norm_rows, hidden_rows, gain_one, shift_one)
        normed = normed_f.astype(jnp.bfloat16)
        normed_all = lax.all_gather(normed, "tp", axis=0, tiled=True)
        queries = (
            row_product(normed_all, query_w) + query_b.reshape(head_width).astype(jnp.float32)
        ).astype(jnp.bfloat16)
        keys_now = row_product(normed_all, key_w).astype(jnp.bfloat16)
        values_now = (
            row_product(normed_all, value_w) + value_b.reshape(head_width).astype(jnp.float32)
        ).astype(jnp.bfloat16)
        pairs = jnp.concatenate([keys_now, values_now], axis=-1)
        pairs_all = lax.all_gather(pairs, "wide", axis=1, tiled=True)
        totals, summed = lax.map(
            forward_group, (query_view(queries), pair_view(pairs_all), grouped_lengths)
        )
        return (
            normed_all,
            queries,
            pairs_all,
            totals,
            summed.reshape(slot_total, block_len, head_width),
            norm_back,
        )

    forward_parts = attention_forward(hidden)
    attention = forward_parts[4].astype(jnp.bfloat16)
    branch = lax.psum_scatter(
        row_product(attention, dense_w).astype(jnp.bfloat16), "tp", scatter_dimension=0, tiled=True
    ).astype(jnp.float32)
    residual = hidden + branch + dense_b.astype(jnp.float32)
    second_f, second_back = jax.vjp(norm_rows, residual, gain_two, shift_two)
    second = second_f.astype(jnp.bfloat16)
    grad_output = validity[:, :, None] * cotangent.astype(jnp.float32)
    grad_down = grad_output.astype(jnp.bfloat16)
    second_all, grad_down_all = (
        lax.all_gather(second, "tp", axis=0, tiled=True),
        lax.all_gather(grad_down, "tp", axis=0, tiled=True),
    )
    pre_act = row_product(second_all, up_w) + up_b.reshape(-1).astype(jnp.float32)
    act_value, act_back = jax.vjp(activate, pre_act)
    activated = act_value.astype(jnp.bfloat16)
    down_out = lax.psum_scatter(
        row_product(activated, down_w).astype(jnp.bfloat16), "tp", scatter_dimension=0, tiled=True
    ).astype(jnp.float32)
    grad_act = times_transposed(grad_down_all, down_w)
    grad_pre = act_back(grad_act)[0].astype(jnp.bfloat16)
    grad_up = inner_rows(second_all, grad_pre)
    grad_up_b = jnp.sum(flatten_rows(grad_pre), axis=0, dtype=jnp.float32).reshape(up_b.shape)
    grad_down_w = inner_rows(activated, grad_down_all)
    grad_second = lax.psum_scatter(
        times_transposed(grad_pre, up_w), "tp", scatter_dimension=0, tiled=True
    )
    output = (validity[:, :, None] * (residual + down_out + down_b.astype(jnp.float32))).astype(
        jnp.bfloat16
    )
    grad_resid_norm, grad_gain_two, grad_shift_two = second_back(grad_second)
    grad_resid = grad_output + grad_resid_norm
    grad_branch = grad_resid.astype(jnp.bfloat16)
    hidden_again, grad_branch = lax.optimization_barrier((hidden, grad_branch))
    forward_parts = attention_forward(hidden_again)
    normed_all, queries, pairs_all, totals, summed, norm_back = forward_parts
    attention_back = summed.astype(jnp.bfloat16)
    branch_all = lax.all_gather(grad_branch, "tp", axis=0, tiled=True)
    grad_dense_w = inner_rows(attention_back, branch_all)
    grad_attention = times_transposed(branch_all, dense_w).astype(jnp.bfloat16)

    def backward_group(inputs):
        query_blk, pair_blk, lengths_blk, totals_blk, grad_blk = inputs
        masked = masked_scores(
            query_blk, pair_blk[:, :, 0], lengths_blk, slopes, distance, causal_mask, key_places
        )
        probabilities = jnp.exp(masked - totals_blk[..., None])
        grad_probs = jnp.einsum(
            "gihd,gjhd->ghij", grad_blk, pair_blk[:, :, 1], preferred_element_type=jnp.float32
        )
        row_delta = jnp.sum(probabilities * grad_probs, axis=-1, keepdims=True)
        grad_scores = (probabilities * (grad_probs - row_delta)).astype(jnp.bfloat16)
        grad_query = (
            jnp.einsum(
                "ghij,gjhd->gihd",
                grad_scores,
                pair_blk[:, :, 0],
                preferred_element_type=jnp.float32,
            )
            * 0.125
        )
        grad_key = (
            jnp.einsum(
                "ghij,gihd->gjhd", grad_scores, query_blk, preferred_element_type=jnp.float32
            )
            * 0.125
        )
        grad_value = jnp.einsum(
            "ghij,gihd->gjhd",
            probabilities.astype(jnp.bfloat16),
            grad_blk,
            preferred_element_type=jnp.float32,
        )
        return (grad_query, jnp.stack([grad_key, grad_value], axis=2))

    grad_query_all, grad_pairs = lax.map(
        backward_group,
        (
            query_view(queries),
            pair_view(pairs_all),
            grouped_lengths,
            totals,
            query_view(grad_attention),
        ),
    )
    grad_pairs_local = lax.psum_scatter(
        grad_pairs.reshape(slot_total, slot_len, 2 * head_width).astype(jnp.bfloat16),
        "wide",
        scatter_dimension=1,
        tiled=True,
    ).astype(jnp.float32)
    grad_queries = grad_query_all.reshape(slot_total, block_len, head_width).astype(jnp.bfloat16)
    grad_keys = grad_pairs_local[:, :, :head_width].astype(jnp.bfloat16)
    grad_values = grad_pairs_local[:, :, head_width:].astype(jnp.bfloat16)
    grad_query_w = inner_rows(normed_all, grad_queries)
    grad_key_w = inner_rows(normed_all, grad_keys)
    grad_value_w = inner_rows(normed_all, grad_values)
    grad_query_b = jnp.sum(flatten_rows(grad_queries), axis=0, dtype=jnp.float32).reshape(
        heads_dev, HEAD
    )
    grad_value_b = jnp.sum(flatten_rows(grad_values), axis=0, dtype=jnp.float32).reshape(
        heads_dev, HEAD
    )
    grad_normed = lax.psum_scatter(
        (
            times_transposed(grad_queries, query_w)
            + times_transposed(grad_keys, key_w)
            + times_transposed(grad_values, value_w)
        ).astype(jnp.bfloat16),
        "tp",
        scatter_dimension=0,
        tiled=True,
    ).astype(jnp.float32)
    grad_hidden_norm, grad_gain_one, grad_shift_one = norm_back(grad_normed)
    grad_in = (grad_resid + grad_hidden_norm).astype(jnp.bfloat16)
    (
        sum_query_w,
        sum_key_w,
        sum_value_w,
        sum_query_b,
        sum_value_b,
        sum_dense_w,
        sum_up_w,
        sum_up_b,
        sum_down_w,
    ) = (
        lax.psum_scatter(
            grad_query_w.astype(jnp.bfloat16), "wide", scatter_dimension=0, tiled=True
        ).astype(jnp.float32),
        lax.psum_scatter(
            grad_key_w.astype(jnp.bfloat16), "wide", scatter_dimension=0, tiled=True
        ).astype(jnp.float32),
        lax.psum_scatter(
            grad_value_w.astype(jnp.bfloat16), "wide", scatter_dimension=0, tiled=True
        ).astype(jnp.float32),
        lax.psum_scatter(
            grad_query_b.astype(jnp.bfloat16), "wide", scatter_dimension=1, tiled=True
        ).astype(jnp.float32),
        lax.psum_scatter(
            grad_value_b.astype(jnp.bfloat16), "wide", scatter_dimension=1, tiled=True
        ).astype(jnp.float32),
        lax.psum_scatter(
            grad_dense_w.astype(jnp.bfloat16), "wide", scatter_dimension=1, tiled=True
        ).astype(jnp.float32),
        lax.psum_scatter(
            grad_up.astype(jnp.bfloat16), "wide", scatter_dimension=0, tiled=True
        ).astype(jnp.float32),
        lax.psum_scatter(
            grad_up_b.astype(jnp.bfloat16), "wide", scatter_dimension=1, tiled=True
        ).astype(jnp.float32),
        lax.psum_scatter(
            grad_down_w.astype(jnp.bfloat16), "wide", scatter_dimension=1, tiled=True
        ).astype(jnp.float32),
    )
    grad_dense_b = jnp.sum(grad_resid, axis=(0, 1))
    grad_down_b = jnp.sum(grad_output, axis=(0, 1))
    sum_gain_one, sum_shift_one, sum_dense_b, sum_gain_two, sum_shift_two, sum_down_b = lax.psum(
        (grad_gain_one, grad_shift_one, grad_dense_b, grad_gain_two, grad_shift_two, grad_down_b),
        ("wide", "tp"),
    )

    def own_part(tensor):
        return lax.dynamic_slice_in_dim(tensor, wide_at * vec_part, vec_part, 0)

    return (
        output,
        grad_in,
        own_part(sum_gain_one),
        own_part(sum_shift_one),
        sum_query_w,
        sum_key_w,
        sum_value_w,
        sum_query_b,
        sum_value_b,
        sum_dense_w,
        own_part(sum_dense_b),
        own_part(sum_gain_two),
        own_part(sum_shift_two),
        sum_up_w,
        sum_up_b,
        sum_down_w,
        own_part(sum_down_b),
    )


def solution(mesh):
    return jax.shard_map(
        per_device,
        mesh=mesh,
        in_specs=(
            P("tp", "wide", None),
            P(),
            P("wide"),
            P("wide"),
            P("wide", "tp"),
            P("wide", "tp"),
            P("wide", "tp"),
            P("tp", "wide"),
            P("tp", "wide"),
            P("tp", "wide"),
            P("wide"),
            P("wide"),
            P("wide"),
            P("wide", "tp"),
            P("tp", "wide"),
            P("tp", "wide"),
            P("wide"),
            P("tp", "wide", None),
        ),
        out_specs=(
            P("tp", "wide", None),
            P("tp", "wide", None),
            P("wide"),
            P("wide"),
            P("wide", "tp"),
            P("wide", "tp"),
            P("wide", "tp"),
            P("tp", "wide"),
            P("tp", "wide"),
            P("tp", "wide"),
            P("wide"),
            P("wide"),
            P("wide"),
            P("wide", "tp"),
            P("tp", "wide"),
            P("tp", "wide"),
            P("wide"),
        ),
        check_vma=False,
    )
```

profile of v0, /device:TPU:0, one launch (start us, length us, event | category | flops | bytes accessed | tf_op | source)
XLA Modules:
  0.0 1197.6 jit_solution(1751168843750282210)
XLA Ops:
  9.8 10.4 all-gather
  20.2 8.6 all-gather.1
  31.0 8.1 all-gather.2
  39.3 9.7 all_gather.69
  48.9 9.2 all_gather.70
  58.1 19.0 %all-gather.19.cloned.1.call-done = bf16[8,128,1024]{2,1,0:T(8,128)(2,1)} async-done(((bf16[2,128,1024]{2,1,0:T(8,128)(2,1)}), bf16[8,128,1024]{2,1,0:T(8,128)(2,1)}) %all-gather.19.cloned.1.call-update) | async-done | bytes 2097168 | tf_op jit(solution)/shard_map/all_gather | solution.py:157
  83.0 8.8 all-gather.3
  92.0 12.5 %all_gather.73 = bf16[1024,256]{1,0:T(8,128)(2,1)S(1)} all-gather(bf16[128,256]{1,0:T(8,128)(2,1)S(1)} %copy-done.28), channel_id=1, replica_groups=mesh['wide'=8,'tp'=4] {'wide'}, dimensions={0}, use_global_device_ids=true | all-gather | bytes 589824 | tf_op jit(solution)/shard_map/all_gather | solution.py:104
  104.5 9.7 all_gather.75
  117.0 21.2 %all-gather.21.cloned.1.call-done = bf16[8,1024,512]{2,1,0:T(8,128)(2,1)} async-done(((bf16[8,128,512]{2,1,0:T(8,128)(2,1)}), bf16[8,1024,512]{2,1,0:T(8,128)(2,1)}) %all-gather.21.cloned.1.call-update) | async-done | bytes 8388624 | tf_op jit(solution)/shard_map/all_gather | solution.py:166
  138.2 11.5 copy.94
  149.8 21.8 %while.40 = (s32[]{:T(128)}, bf16[2,4,128,4,64]{2,4,3,1,0:T(8,128)(2,1)S(1)}, bf16[2,4,1024,2,4,64]{2,5,4,3,1,0:T(8,128)(2,1)}, s32[2,4]{1,0:T(2,128)S(1)}, bf16...) while((s32[]{:T(128)}, ...), condition=%wide.region_5.6_spmd.clone.clone, body=%wide.region_2.5_spmd.clone.clone.sunk | while | flops 567674880 | bytes 50398400 | solution.py:167
  174.4 8.7 all-gather.4
  183.1 7.8 all-gather.5
  191.0 8.7 all-gather.6
  199.7 17.8 %reduce-scatter.21.cloned.1.call-done = bf16[2,128,1024]{2,1,0:T(8,128)(2,1)} async-done(((bf16[8,128,1024]{2,1,0:T(8,128)(2,1)}), bf16[2,128,1024]{2,1,0:T(8,128)(2,1)}) %reduce-scatter.21.cloned.1.call-update) | async-done | bytes 524304 | tf_op jit(solution)/shard_map/reduce_scatter | solution.py:181
  224.4 9.1 all-gather.7
  233.5 12.8 %all-gather.25.cloned.1.call-done = bf16[1024,1024]{1,0:T(8,128)(2,1)} async-done(((bf16[128,1024]{1,0:T(8,128)(2,1)}), bf16[1024,1024]{1,0:T(8,128)(2,1)}) %all-gather.25.cloned.1.call-update) | async-done | bytes 2097168 | tf_op jit(solution)/shard_map/all_gather | solution.py:113
  246.3 47.7 %all-gather.23.cloned.1.call-done = bf16[8,128,1024]{2,1,0:T(8,128)(2,1)} async-done(((bf16[2,128,1024]{2,1,0:T(8,128)(2,1)}), bf16[8,128,1024]{2,1,0:T(8,128)(2,1)}) %all-gather.23.cloned.1.call-update) | async-done | bytes 2097168 | tf_op jit(solution)/shard_map/all_gather | solution.py:190
  294.0 6.5 fusion.83
  300.6 40.0 %all-gather.29.cloned.1.call-done = bf16[8,128,1024]{2,1,0:T(8,128)(2,1)} async-done(((bf16[2,128,1024]{2,1,0:T(8,128)(2,1)}), bf16[8,128,1024]{2,1,0:T(8,128)(2,1)}) %all-gather.29.cloned.1.call-update) | async-done | bytes 2097168 | tf_op jit(solution)/shard_map/all_gather | solution.py:191
  340.5 28.8 %all-gather.27.cloned.1.call-done = bf16[1024,1024]{1,0:T(8,128)(2,1)} async-done(((bf16[1024,128]{1,0:T(8,128)(2,1)}), bf16[1024,1024]{1,0:T(8,128)(2,1)}) %all-gather.27.cloned.1.call-update) | async-done | bytes 2097168 | tf_op jit(solution)/shard_map/all_gather | solution.py:115
  369.3 8.9 fusion.127
  384.0 7.1 fusion.85
  391.3 9.0 all-gather.8
  400.3 60.6 %reduce-scatter.25.cloned.1.call-done = f32[2,128,1024]{2,1,0:T(8,128)} async-done(((f32[8,128,1024]{2,1,0:T(8,128)}), f32[2,128,1024]{2,1,0:T(8,128)}) %reduce-scatter.25.cloned.1.call-update) | async-done | bytes 1048592 | tf_op jit(solution)/shard_map/reduce_scatter | solution.py:204
  463.2 44.1 %reduce-scatter.23.cloned.1.call-done = bf16[2,128,1024]{2,1,0:T(8,128)(2,1)} async-done(((bf16[8,128,1024]{2,1,0:T(8,128)(2,1)}), bf16[2,128,1024]{2,1,0:T(8,128)(2,1)}) %reduce-scatter.23.cloned.1.call-update) | async-done | bytes 524304 | tf_op jit(solution)/shard_map/reduce_scatter | solution.py:196
  514.5 44.2 %all-gather.31.cloned.1.call-done = bf16[8,128,1024]{2,1,0:T(8,128)(2,1)} async-done(((bf16[2,128,1024]{2,1,0:T(8,128)(2,1)}), bf16[8,128,1024]{2,1,0:T(8,128)(2,1)}) %all-gather.31.cloned.1.call-update) | async-done | bytes 2097168 | tf_op jit(solution)/shard_map/all_gather | solution.py:157
  564.6 40.7 %all-gather.35.cloned.1.call-done = bf16[8,128,1024]{2,1,0:T(8,128)(2,1)} async-done(((bf16[2,128,1024]{2,1,0:T(8,128)(2,1)}), bf16[8,128,1024]{2,1,0:T(8,128)(2,1)}) %all-gather.35.cloned.1.call-update) | async-done | bytes 2097168 | tf_op jit(solution)/shard_map/all_gather | solution.py:217
  610.6 49.6 %all-gather.33.cloned.1.call-done = bf16[8,1024,512]{2,1,0:T(8,128)(2,1)} async-done(((bf16[8,128,512]{2,1,0:T(8,128)(2,1)}), bf16[8,1024,512]{2,1,0:T(8,128)(2,1)}) %all-gather.33.cloned.1.call-update) | async-done | bytes 8388624 | tf_op jit(solution)/shard_map/all_gather | solution.py:166
  660.2 11.5 copy.100
  671.7 8.4 copy.104
  680.3 21.9 %while.41 = (s32[]{:T(128)}, f32[2,4,4,128]{3,2,1,0:T(4,128)S(1)}, bf16[2,4,128,4,64]{2,4,3,1,0:T(8,128)(2,1)S(1)}, s32[2,4]{1,0:T(2,128)S(1)}, bf16[2,4,128,4,6...) while((s32[]{:T(128)}, f32[2,4,4,128]{3,2,1,0:T(4,128)S(1)}, ...), condition=%wide.region_18.19_spmd.clone.clone, body=%wide.region_15.18_spmd.clone.clone.sunk | while | flops 567674880 | bytes 50406604 | solution.py:167
  703.1 35.1 %while.42 = (s32[]{:T(128)}, bf16[2,4,128,4,64]{2,4,3,1,0:T(8,128)(2,1)}, bf16[2,4,1024,2,4,64]{2,5,4,3,1,0:T(8,128)(2,1)}, bf16[2,4,1024,2,4,64]{2,5,4,1,3,0:T(...) while((s32[]{:T(128)}, ...), condition=%wide.region_21.22_spmd.clone.clone, body=%wide.region_19.21_spmd.clone.clone.sunk | while | flops 1368918016 | bytes 161269104 | solution.py:255
  738.2 11.4 copy.107
  751.2 5.9 bitcast_convert_fusion
  760.0 6.8 bitcast_convert_fusion.1
  773.6 47.6 %reduce-scatter.27.cloned.1.call-done = bf16[8,128,512]{2,1,0:T(8,128)(2,1)} async-done(((bf16[8,1024,512]{2,1,0:T(8,128)(2,1)}), bf16[8,128,512]{2,1,0:T(8,128)(2,1)}) %reduce-scatter.27.cloned.1.call-update) | async-done | bytes 1048592 | tf_op jit(solution)/shard_map/reduce_scatter | solution.py:265
  834.8 23.4 %reduce-scatter.41.cloned.1.call-done = bf16[32,4]{1,0:T(8,128)(2,1)} async-done(((bf16[256,4]{1,0:T(8,128)(2,1)}), bf16[32,4]{1,0:T(8,128)(2,1)}) %reduce-scatter.41.cloned.1.call-update) | async-done | bytes 272
  859.5 42.9 %reduce-scatter.43.cloned.1.call-done = bf16[128,1024]{1,0:T(8,128)(2,1)} async-done(((bf16[1024,1024]{1,0:T(8,128)(2,1)}), bf16[128,1024]{1,0:T(8,128)(2,1)}) %reduce-scatter.43.cloned.1.call-update) | async-done | bytes 262160
  904.4 42.3 %reduce-scatter.37.cloned.1.call-done = bf16[128,1024]{1,0:T(8,128)(2,1)} async-done(((bf16[1024,1024]{1,0:T(8,128)(2,1)}), bf16[128,1024]{1,0:T(8,128)(2,1)}) %reduce-scatter.37.cloned.1.call-update) | async-done | bytes 262160 | tf_op jit(solution)/shard_map/reduce_scatter | solution.py:324
  948.6 35.2 %reduce-scatter.39.cloned.1.call-done = bf16[128,256]{1,0:T(8,128)(2,1)} async-done(((bf16[1024,256]{1,0:T(8,128)(2,1)}), bf16[128,256]{1,0:T(8,128)(2,1)}) %reduce-scatter.39.cloned.1.call-update) | async-done | bytes 65552
  985.4 35.5 %reduce-scatter.31.cloned.1.call-done = bf16[128,256]{1,0:T(8,128)(2,1)} async-done(((bf16[1024,256]{1,0:T(8,128)(2,1)}), bf16[128,256]{1,0:T(8,128)(2,1)}) %reduce-scatter.31.cloned.1.call-update) | async-done | bytes 65552 | tf_op jit(solution)/shard_map/reduce_scatter | solution.py:306
  1023.7 12.1 %all-reduce.3 = (bf16[4,64]{1,0:T(4,128)(2,1)S(1)}, bf16[4,64]{1,0:T(4,128)(2,1)S(1)}) all-reduce(bf16[4,64]{1,0:T(4,128)(2,1)S(1)} %reduce_sum.251, bf16[4,64]{1,0:T(4,128)(2,1)S(1)} %convert_element_type.288), channel_id=10, replica_groups=mesh['wide'=8,'tp'=4] {'wide'}, use_global_device_ids=true, to_apply=%region_34.35.clone | all-reduce | flops 512 | bytes 2048
  1036.5 21.7 %reduce-scatter.35.cloned.1.call-done = bf16[128,256]{1,0:T(8,128)(2,1)} async-done(((bf16[1024,256]{1,0:T(8,128)(2,1)}), bf16[128,256]{1,0:T(8,128)(2,1)}) %reduce-scatter.35.cloned.1.call-update) | async-done | bytes 65552 | tf_op jit(solution)/shard_map/reduce_scatter | solution.py:312
  1059.7 36.2 %reduce-scatter.33.cloned.1.call-done = bf16[128,256]{1,0:T(8,128)(2,1)} async-done(((bf16[1024,256]{1,0:T(8,128)(2,1)}), bf16[128,256]{1,0:T(8,128)(2,1)}) %reduce-scatter.33.cloned.1.call-update) | async-done | bytes 65552 | tf_op jit(solution)/shard_map/reduce_scatter | solution.py:309
  1097.4 44.5 %reduce-scatter.29.cloned.1.call-done = bf16[2,128,1024]{2,1,0:T(8,128)(2,1)} async-done(((bf16[8,128,1024]{2,1,0:T(8,128)(2,1)}), bf16[2,128,1024]{2,1,0:T(8,128)(2,1)}) %reduce-scatter.29.cloned.1.call-update) | async-done | bytes 524304 | tf_op jit(solution)/shard_map/reduce_scatter | solution.py:283
  1147.3 39.7 %all-reduce.2 = (f32[1024]{0:T(1024)S(1)}, f32[1024]{0:T(1024)S(1)}, f32[1024]{0:T(1024)S(1)}, f32[1024]{0:T(1024)S(1)}, f32[1024]{0:T(1024)S(1)}, /*index=5*/f32[1024]{0:T(1024)S(1)}) all-reduce(f32[1024]{0:T(1024)S(1)} %get-tuple-element.442, f32[1024]{0:T(1024)S(1)} %get-tuple-element.447, ...), channel_id=1, replica_groups=mesh['wide'=8,'tp'=4] {'wide','tp'}, use_global_device_ids=true, to_apply=%region_27.28 | all-reduce | flops 6144 | bytes 49152 | tf_op jit(solution)/shard_map/psum | solution.py:336
  (347 shorter events, 174.5 us)
Async XLA Ops:
  7.2 69.9 %all-gather.19.cloned.1.call-start = ((), (), s32[]{:S(2)}) async-start(), calls=%async_computation.12 | async-start | bytes 2621440 | tf_op jit(solution)/shard_map/all_gather | solution.py:157
  20.2 492.4 %copy-start.26 = (f32[8,1,128]{2,1,0:T(1,128)}, f32[8,1,128]{2,1,0:T(1,128)S(1)}, u32[]{:S(2)}) copy-start(f32[8,1,128]{2,1,0:T(1,128)S(1)} %convert_element_type.303) | copy-start | bytes 12292
  30.9 107.2 %all-gather.21.cloned.1.call-start = ((), (), s32[]{:S(2)}) async-start(), calls=%async_computation.13 | async-start | bytes 9437184 | tf_op jit(solution)/shard_map/all_gather | solution.py:166
  58.1 502.9 %copy-start.14 = (bf16[1024,256]{1,0:T(8,128)(2,1)}, bf16[1024,256]{1,0:T(8,128)(2,1)S(1)}, u32[]{:S(2)}) copy-start(bf16[1024,256]{1,0:T(8,128)(2,1)S(1)} %all_gather.70) | copy-start | bytes 1572868
  82.9 134.6 %reduce-scatter.21.cloned.1.call-start = ((), (), s32[]{:S(2)}) async-start(), calls=%async_computation.14 | async-start | bytes 2621440 | tf_op jit(solution)/shard_map/reduce_scatter | solution.py:181
  114.2 57.5 %copy-start.22 = (bf16[256,1024]{1,0:T(8,128)(2,1)}, bf16[256,1024]{1,0:T(8,128)(2,1)S(1)}, u32[]{:S(2)}) copy-start(bf16[256,1024]{1,0:T(8,128)(2,1)S(1)} %all_gather.75) | copy-start | bytes 1572868
  171.6 45.9 %copy-start.2 = (bf16[2,128,1024]{2,1,0:T(8,128)(2,1)S(1)}, bf16[2,128,1024]{2,1,0:T(8,128)(2,1)}, u32[]{:S(2)}) copy-start(bf16[2,128,1024]{2,1,0:T(8,128)(2,1)} %param.24) | copy-start | bytes 1572868
  171.7 50.9 %copy-start.8 = (bf16[2,128,1024]{2,1,0:T(8,128)(2,1)S(1)}, bf16[2,128,1024]{2,1,0:T(8,128)(2,1)}, u32[]{:S(2)}) copy-start(bf16[2,128,1024]{2,1,0:T(8,128)(2,1)} %param.41) | copy-start | bytes 1572868
  173.7 50.7 %copy-start.46 = (bf16[4,32]{1,0:T(4,128)(2,1)S(1)}, bf16[4,32]{1,0:T(4,128)(2,1)}, u32[]{:S(2)}) copy-start(bf16[4,32]{1,0:T(4,128)(2,1)} %param.38) | copy-start | bytes 772
  173.7 72.6 %all-gather.25.cloned.1.call-start = ((), (), s32[]{:S(2)}) async-start(), calls=%async_computation.16 | async-start | bytes 2359296 | tf_op jit(solution)/shard_map/all_gather | solution.py:113
  174.3 119.7 %all-gather.23.cloned.1.call-start = ((), (), s32[]{:S(2)}) async-start(), calls=%async_computation.15 | async-start | bytes 2621440 | tf_op jit(solution)/shard_map/all_gather | solution.py:190
  222.4 118.1 %all-gather.29.cloned.1.call-start = ((), (), s32[]{:S(2)}) async-start(), calls=%async_computation.19 | async-start | bytes 2621440 | tf_op jit(solution)/shard_map/all_gather | solution.py:191
  222.6 287.5 %copy-start.32 = (f32[2,128]{1,0:T(2,128)}, f32[2,128]{1,0:T(2,128)S(1)}, u32[]{:S(2)}) copy-start(f32[2,128]{1,0:T(2,128)S(1)} %compare_convert_fusion) | copy-start | bytes 3076
  223.6 145.8 %all-gather.27.cloned.1.call-start = ((), (), s32[]{:S(2)}) async-start(), calls=%async_computation.17 | async-start | bytes 2359296 | tf_op jit(solution)/shard_map/all_gather | solution.py:115
  224.3 236.6 %reduce-scatter.25.cloned.1.call-start = ((), (), s32[]{:S(2)}) async-start(), calls=%async_computation.20 | async-start | bytes 5242880 | tf_op jit(solution)/shard_map/reduce_scatter | solution.py:204
  233.5 150.5 %copy-start.42 = (f32[1,2,4,128]{3,1,2,0:T(2,128)}, f32[1,2,4,128]{3,1,2,0:T(2,128)S(1)}, u32[]{:S(2)}) copy-start(f32[1,2,4,128]{3,1,2,0:T(2,128)S(1)} %copy.151) | copy-start | bytes 12292
  384.0 76.9 %copy-start.4 = (bf16[2,128,1024]{2,1,0:T(8,128)(2,1)S(1)}, bf16[2,128,1024]{2,1,0:T(8,128)(2,1)}, u32[]{:S(2)}) copy-start(bf16[2,128,1024]{2,1,0:T(8,128)(2,1)} %reduce-scatter.21.cloned.1.call-done) | copy-start | bytes 1572868
  384.0 123.4 %reduce-scatter.23.cloned.1.call-start = ((), (), s32[]{:S(2)}) async-start(), calls=%async_computation.18 | async-start | bytes 2621440 | tf_op jit(solution)/shard_map/reduce_scatter | solution.py:196
  391.1 167.6 %all-gather.31.cloned.1.call-start = ((), (), s32[]{:S(2)}) async-start(), calls=%async_computation.21 | async-start | bytes 2621440 | tf_op jit(solution)/shard_map/all_gather | solution.py:157
  391.3 121.3 %copy-start = (f32[2,128,1024]{2,1,0:T(8,128)}, f32[2,128,1024]{2,1,0:T(8,128)S(1)}, u32[]{:S(2)}) copy-start(f32[2,128,1024]{2,1,0:T(8,128)S(1)} %convert_element_type.237) | copy-start | bytes 3145732
  510.1 48.6 %copy-start.17 = (bf16[1024,256]{1,0:T(8,128)(2,1)S(1)}, bf16[1024,256]{1,0:T(8,128)(2,1)}, u32[]{:S(2)}) copy-start(bf16[1024,256]{1,0:T(8,128)(2,1)} %copy-done.16) | copy-start | bytes 1572868
  512.3 51.1 %copy-start.30 = (f32[2,128]{1,0:T(2,128)}, f32[2,128]{1,0:T(2,128)S(1)}, u32[]{:S(2)}) copy-start(f32[2,128]{1,0:T(2,128)S(1)} %broadcast_multiply_fusion.3) | copy-start | bytes 3076
  512.6 48.5 %copy-start.40 = (f32[2,128]{1,0:T(2,128)}, f32[2,128]{1,0:T(2,128)S(1)}, u32[]{:S(2)}) copy-start(f32[2,128]{1,0:T(2,128)S(1)} %multiply_reduce_fusion.2) | copy-start | bytes 3076
  512.6 50.8 %copy-start.34 = (f32[2,128]{1,0:T(2,128)}, f32[2,128]{1,0:T(2,128)S(1)}, u32[]{:S(2)}) copy-start(f32[2,128]{1,0:T(2,128)S(1)} %fusion.125) | copy-start | bytes 3076
  513.7 91.7 %all-gather.35.cloned.1.call-start = ((), (), s32[]{:S(2)}) async-start(), calls=%async_computation.23 | async-start | bytes 2621440 | tf_op jit(solution)/shard_map/all_gather | solution.py:217
  514.4 145.8 %all-gather.33.cloned.1.call-start = ((), (), s32[]{:S(2)}) async-start(), calls=%async_computation.22 | async-start | bytes 9437184 | tf_op jit(solution)/shard_map/all_gather | solution.py:166
  563.4 44.5 %copy-start.20 = (bf16[1024,256]{1,0:T(8,128)(2,1)S(1)}, bf16[1024,256]{1,0:T(8,128)(2,1)}, u32[]{:S(2)}) copy-start(bf16[1024,256]{1,0:T(8,128)(2,1)} %copy-done.19) | copy-start | bytes 1572868
  564.6 256.6 %reduce-scatter.27.cloned.1.call-start = ((), (), s32[]{:S(2)}) async-start(), calls=%async_computation.24 | async-start | bytes 9437184 | tf_op jit(solution)/shard_map/reduce_scatter | solution.py:265
  749.6 108.5 %reduce-scatter.41.cloned.1.call-start = ((), (), s32[]{:S(2)}) async-start(), calls=%async_computation.31 | async-start | bytes 73728
  751.1 151.3 %reduce-scatter.43.cloned.1.call-start = ((), (), s32[]{:S(2)}) async-start(), calls=%async_computation.32 | async-start | bytes 2359296
  759.9 186.7 %reduce-scatter.37.cloned.1.call-start = ((), (), s32[]{:S(2)}) async-start(), calls=%async_computation.29 | async-start | bytes 2359296 | tf_op jit(solution)/shard_map/reduce_scatter | solution.py:324
  766.8 217.0 %reduce-scatter.39.cloned.1.call-start = ((), (), s32[]{:S(2)}) async-start(), calls=%async_computation.30 | async-start | bytes 589824
  770.3 250.6 %reduce-scatter.31.cloned.1.call-start = ((), (), s32[]{:S(2)}) async-start(), calls=%async_computation.26 | async-start | bytes 589824 | tf_op jit(solution)/shard_map/reduce_scatter | solution.py:306
  773.5 51.0 %copy-start.21 = (bf16[1024,256]{1,0:T(8,128)(2,1)S(1)}, bf16[1024,256]{1,0:T(8,128)(2,1)}, u32[]{:S(2)}) copy-start(bf16[1024,256]{1,0:T(8,128)(2,1)} %copy-done.19) | copy-start | bytes 1572868
  773.5 284.6 %reduce-scatter.35.cloned.1.call-start = ((), (), s32[]{:S(2)}) async-start(), calls=%async_computation.28 | async-start | bytes 589824 | tf_op jit(solution)/shard_map/reduce_scatter | solution.py:312
  824.4 271.4 %reduce-scatter.33.cloned.1.call-start = ((), (), s32[]{:S(2)}) async-start(), calls=%async_computation.27 | async-start | bytes 589824 | tf_op jit(solution)/shard_map/reduce_scatter | solution.py:309
  828.8 313.0 %reduce-scatter.29.cloned.1.call-start = ((), (), s32[]{:S(2)}) async-start(), calls=%async_computation.25 | async-start | bytes 2621440 | tf_op jit(solution)/shard_map/reduce_scatter | solution.py:283
  833.3 308.6 %copy-start.1 = (f32[2,128,1024]{2,1,0:T(8,128)S(1)}, f32[2,128,1024]{2,1,0:T(8,128)}, u32[]{:S(2)}) copy-start(f32[2,128,1024]{2,1,0:T(8,128)} %copy-done) | copy-start | bytes 3145732
  833.3 308.6 %copy-start.27 = (f32[8,1,128]{2,1,0:T(1,128)S(1)}, f32[8,1,128]{2,1,0:T(1,128)}, u32[]{:S(2)}) copy-start(f32[8,1,128]{2,1,0:T(1,128)} %copy-done.26) | copy-start | bytes 12292
  833.3 308.6 %copy-start.31 = (f32[2,128]{1,0:T(2,128)S(1)}, f32[2,128]{1,0:T(2,128)}, u32[]{:S(2)}) copy-start(f32[2,128]{1,0:T(2,128)} %copy-done.30) | copy-start | bytes 3076
  833.3 309.9 %copy-start.41 = (f32[2,128]{1,0:T(2,128)S(1)}, f32[2,128]{1,0:T(2,128)}, u32[]{:S(2)}) copy-start(f32[2,128]{1,0:T(2,128)} %copy-done.40) | copy-start | bytes 3076
  833.3 309.9 %copy-start.35 = (f32[2,128]{1,0:T(2,128)S(1)}, f32[2,128]{1,0:T(2,128)}, u32[]{:S(2)}) copy-start(f32[2,128]{1,0:T(2,128)} %copy-done.34) | copy-start | bytes 3076
  833.3 311.5 %copy-start.6 = (f32[2,128,1024]{2,1,0:T(8,128)S(1)}, f32[2,128,1024]{2,1,0:T(8,128)}, u32[]{:S(2)}) copy-start(f32[2,128,1024]{2,1,0:T(8,128)} %copy-done.5) | copy-start | bytes 3145732
  833.3 311.5 %copy-start.9 = (bf16[2,128,1024]{2,1,0:T(8,128)(2,1)S(1)}, bf16[2,128,1024]{2,1,0:T(8,128)(2,1)}, u32[]{:S(2)}) copy-start(bf16[2,128,1024]{2,1,0:T(8,128)(2,1)} %param.41) | copy-start | bytes 1572868
  833.3 311.5 %copy-start.33 = (f32[2,128]{1,0:T(2,128)S(1)}, f32[2,128]{1,0:T(2,128)}, u32[]{:S(2)}) copy-start(f32[2,128]{1,0:T(2,128)} %copy-done.32) | copy-start | bytes 3076
  833.3 311.5 %copy-start.39 = (f32[2,128]{1,0:T(2,128)S(1)}, f32[2,128]{1,0:T(2,128)}, u32[]{:S(2)}) copy-start(f32[2,128]{1,0:T(2,128)} %copy-done.38) | copy-start | bytes 3076
  948.6 198.7 %copy-start.36 = (f32[1024]{0:T(1024)S(1)}, f32[1024]{0:T(1024)}, u32[]{:S(2)}) copy-start(f32[1024]{0:T(1024)} %get-tuple-element.440) | copy-start | bytes 12292
  948.6 198.7 %copy-start.37 = (f32[1024]{0:T(1024)S(1)}, f32[1024]{0:T(1024)}, u32[]{:S(2)}) copy-start(f32[1024]{0:T(1024)} %get-tuple-element.444) | copy-start | bytes 12292
  (36 other events, 239.6 us)
Sparse Core Ops, SparseCore 0:
  31.1 45.9 all-gather.18
  83.0 55.0 all-gather.20
  173.9 43.6 reduce-scatter.20
  219.3 27.0 all-gather.24
  248.3 45.6 all-gather.22
  296.0 44.4 all-gather.28
  342.4 26.8 all-gather.26
  384.1 76.7 reduce-scatter.24
  463.2 44.0 reduce-scatter.22
  513.8 44.8 all-gather.30
  560.9 44.4 all-gather.34
  607.1 53.0 all-gather.32
  749.8 71.3 reduce-scatter.26
  824.6 33.5 reduce-scatter.40
  861.3 41.0 reduce-scatter.42
  905.6 41.0 reduce-scatter.36
  949.6 34.1 reduce-scatter.38
  986.7 34.1 reduce-scatter.30
  1024.0 34.1 reduce-scatter.34
  1061.7 34.1 reduce-scatter.32
  1098.2 43.6 reduce-scatter.28
where the time goes:
time: 1200 us
  waiting for transfers between devices  758 us (63%)
  blocking collectives  172 us (14%)
  matrix products  108 us (9%)
  local copies, waits for them, and re-layouts  86.3 us (7%)
  other arithmetic  54.7 us (5%)
  between operations  16.1 us (1%)
    unnamed x24, waiting for transfers between devices  104 us
    all_gather x2, waiting for transfers between devices, attention_forward(): pairs_all = lax.all_gather(pairs, 'wide', axis=1, tiled=True)  70.8 us
    all_gather x2, waiting for transfers between devices, attention_forward(): normed_all = lax.all_gather(normed, 'tp', axis=0, tiled=True)  63.2 us
    reduce_scatter x1, waiting for transfers between devices, per_device(): lax.psum_scatter(times_transposed(grad_pre, up_w), 'tp', scatter_dimensio...  60.6 us
    all_gather x1, waiting for transfers between devices, per_device(): lax.all_gather(second, 'tp', axis=0, tiled=True)  47.7 us
    reduce_scatter x1, waiting for transfers between devices, per_device(): lax.psum_scatter(grad_pairs.reshape(slot_total, slot_len, 2 * head_width)...  47.6 us
    reduce_scatter x1, waiting for transfers between devices, per_device(): lax.psum_scatter((times_transposed(grad_queries, query_w) + times_transpo...  44.5 us
    reduce_scatter x1, waiting for transfers between devices, per_device(): lax.psum_scatter(row_product(activated, down_w).astype(jnp.bfloat16), 'tp...  44.1 us
  transfers between devices with their start and end apart: 21, of which 21 were waited for; matrix products, arithmetic and copies ran while one was open for 7% of the time, Pallas kernels for 0%

commit v1 on v0

--- a/solution.py
+++ b/solution.py
@@ -5,6 +5,18 @@
 from jax.sharding import PartitionSpec as P
 
 HEAD = 64
+
+
+def collect(x, axis, dim):
+    ways, here = (lax.axis_size(axis), lax.axis_index(axis))
+    grown, reach = (x, 1)
+    while reach < ways:
+        theirs = lax.ppermute(grown, axis, [(d, d ^ reach) for d in range(ways)])
+        mine_first = jnp.concatenate([grown, theirs], axis=dim)
+        theirs_first = jnp.concatenate([theirs, grown], axis=dim)
+        grown = jnp.where(here & reach == 0, mine_first, theirs_first)
+        reach = 2 * reach
+    return grown
 
 
 def norm_rows(values, gain_vec, shift_vec):
@@ -214,7 +226,7 @@
     forward_parts = attention_forward(hidden_again)
     normed_all, queries, pairs_all, totals, summed, norm_back = forward_parts
     attention_back = summed.astype(jnp.bfloat16)
-    branch_all = lax.all_gather(grad_branch, "tp", axis=0, tiled=True)
+    branch_all = collect(grad_branch, "tp", 0)
     grad_dense_w = inner_rows(attention_back, branch_all)
     grad_attention = times_transposed(branch_all, dense_w).astype(jnp.bfloat16)
 

time: 1200 us -> 1170 us (0.975)
  waiting for transfers between devices: 758 us -> 726 us
    ppermute x0 -> x2, waiting for transfers between devices: none -> 59.4 us  [collect(): theirs = lax.ppermute(grown, axis, [(d, d ^ reach) for d in range(ways)])]
    all_gather x2, waiting for transfers between devices: 70.8 us -> 21.2 us  [attention_forward(): pairs_all = lax.all_gather(pairs, 'wide', axis=1, tiled=True)]
    all_gather x1 -> x0, waiting for transfers between devices: 40.7 us -> none  [per_device(): branch_all = lax.all_gather(grad_branch, 'tp', axis=0, tiled=True)]
    unnamed x24 -> x23, waiting for transfers between devices: 104 us -> 103 us
  transfers between devices with their start and end apart: 21 -> 22, of which waited for: 21 -> 21; matrix products, arithmetic and copies ran while one was open for 7% -> 7% of each run, Pallas kernels for 0% -> 0%
where the time goes in v1:
time: 1170 us
  waiting for transfers between devices  726 us (62%)
  blocking collectives  172 us (15%)
  matrix products  109 us (9%)
  local copies, waits for them, and re-layouts  86.5 us (7%)
  other arithmetic  54.1 us (5%)
  between operations  16.1 us (1%)
    unnamed x23, waiting for transfers between devices  103 us
    all_gather x2, waiting for transfers between devices, attention_forward(): normed_all = lax.all_gather(normed, 'tp', axis=0, tiled=True)  63.9 us
    reduce_scatter x1, waiting for transfers between devices, per_device(): lax.psum_scatter(times_transposed(grad_pre, up_w), 'tp', scatter_dimensio...  60.4 us
    ppermute x2, waiting for transfers between devices, collect(): theirs = lax.ppermute(grown, axis, [(d, d ^ reach) for d in range(ways)])  59.4 us
    all_gather x1, waiting for transfers between devices, per_device(): lax.all_gather(second, 'tp', axis=0, tiled=True)  47.7 us
    reduce_scatter x1, waiting for transfers between devices, per_device(): lax.psum_scatter(grad_pairs.reshape(slot_total, slot_len, 2 * head_width)...  46.9 us
    reduce_scatter x1, waiting for transfers between devices, per_device(): lax.psum_scatter((times_transposed(grad_queries, query_w) + times_transpo...  44.3 us
    reduce_scatter x1, waiting for transfers between devices, per_device(): lax.psum_scatter(row_product(activated, down_w).astype(jnp.bfloat16), 'tp...  44.1 us
  transfers between devices with their start and end apart: 22, of which 21 were waited for; matrix products, arithmetic and copies ran while one was open for 7% of the time, Pallas kernels for 0%

profile of v1, /device:TPU:0, one launch (start us, length us, event | category | flops | bytes accessed | tf_op | source)
XLA Modules:
  0.0 1166.8 jit_solution(10169743389805605132)
XLA Ops:
  9.8 10.4 all-gather
  20.2 8.6 all-gather.1
  31.0 8.1 all-gather.2
  39.3 9.7 all_gather.66
  48.9 9.2 all_gather.67
  58.1 19.0 %all-gather.18.cloned.1.call-done = bf16[8,128,1024]{2,1,0:T(8,128)(2,1)} async-done(((bf16[2,128,1024]{2,1,0:T(8,128)(2,1)}), bf16[8,128,1024]{2,1,0:T(8,128)(2,1)}) %all-gather.18.cloned.1.call-update) | async-done | bytes 2097168 | tf_op jit(solution)/shard_map/all_gather | solution.py:169
  83.0 8.8 all-gather.3
  92.0 12.5 %all_gather.70 = bf16[1024,256]{1,0:T(8,128)(2,1)S(1)} all-gather(bf16[128,256]{1,0:T(8,128)(2,1)S(1)} %copy-done.30), channel_id=1, replica_groups=mesh['wide'=8,'tp'=4] {'wide'}, dimensions={0}, use_global_device_ids=true | all-gather | bytes 589824 | tf_op jit(solution)/shard_map/all_gather | solution.py:116
  104.5 9.7 all_gather.72
  117.0 21.2 %all-gather.20.cloned.1.call-done = bf16[8,1024,512]{2,1,0:T(8,128)(2,1)} async-done(((bf16[8,128,512]{2,1,0:T(8,128)(2,1)}), bf16[8,1024,512]{2,1,0:T(8,128)(2,1)}) %all-gather.20.cloned.1.call-update) | async-done | bytes 8388624 | tf_op jit(solution)/shard_map/all_gather | solution.py:178
  138.1 11.5 copy.94
  149.8 21.8 %while.40 = (s32[]{:T(128)}, bf16[2,4,128,4,64]{2,4,3,1,0:T(8,128)(2,1)S(1)}, bf16[2,4,1024,2,4,64]{2,5,4,3,1,0:T(8,128)(2,1)}, s32[2,4]{1,0:T(2,128)S(1)}, bf16...) while((s32[]{:T(128)}, ...), condition=%wide.region_5.6_spmd.clone.clone, body=%wide.region_2.5_spmd.clone.clone.sunk | while | flops 567674880 | bytes 50398400 | solution.py:179
  174.4 8.7 all-gather.4
  183.1 7.8 all-gather.5
  191.0 8.7 all-gather.6
  199.7 17.8 %reduce-scatter.21.cloned.1.call-done = bf16[2,128,1024]{2,1,0:T(8,128)(2,1)} async-done(((bf16[8,128,1024]{2,1,0:T(8,128)(2,1)}), bf16[2,128,1024]{2,1,0:T(8,128)(2,1)}) %reduce-scatter.21.cloned.1.call-update) | async-done | bytes 524304 | tf_op jit(solution)/shard_map/reduce_scatter | solution.py:193
  224.4 9.1 all-gather.7
  233.6 12.7 %all-gather.24.cloned.1.call-done = bf16[1024,1024]{1,0:T(8,128)(2,1)} async-done(((bf16[128,1024]{1,0:T(8,128)(2,1)}), bf16[1024,1024]{1,0:T(8,128)(2,1)}) %all-gather.24.cloned.1.call-update) | async-done | bytes 2097168 | tf_op jit(solution)/shard_map/all_gather | solution.py:125
  246.3 47.7 %all-gather.22.cloned.1.call-done = bf16[8,128,1024]{2,1,0:T(8,128)(2,1)} async-done(((bf16[2,128,1024]{2,1,0:T(8,128)(2,1)}), bf16[8,128,1024]{2,1,0:T(8,128)(2,1)}) %all-gather.22.cloned.1.call-update) | async-done | bytes 2097168 | tf_op jit(solution)/shard_map/all_gather | solution.py:202
  294.0 6.5 fusion.83
  300.5 40.0 %all-gather.28.cloned.1.call-done = bf16[8,128,1024]{2,1,0:T(8,128)(2,1)} async-done(((bf16[2,128,1024]{2,1,0:T(8,128)(2,1)}), bf16[8,128,1024]{2,1,0:T(8,128)(2,1)}) %all-gather.28.cloned.1.call-update) | async-done | bytes 2097168 | tf_op jit(solution)/shard_map/all_gather | solution.py:203
  340.5 28.8 %all-gather.26.cloned.1.call-done = bf16[1024,1024]{1,0:T(8,128)(2,1)} async-done(((bf16[1024,128]{1,0:T(8,128)(2,1)}), bf16[1024,1024]{1,0:T(8,128)(2,1)}) %all-gather.26.cloned.1.call-update) | async-done | bytes 2097168 | tf_op jit(solution)/shard_map/all_gather | solution.py:127
  369.3 9.0 fusion.129
  384.0 7.1 fusion.85
  391.3 9.1 all-gather.8
  400.4 60.4 %reduce-scatter.25.cloned.1.call-done = f32[2,128,1024]{2,1,0:T(8,128)} async-done(((f32[8,128,1024]{2,1,0:T(8,128)}), f32[2,128,1024]{2,1,0:T(8,128)}) %reduce-scatter.25.cloned.1.call-update) | async-done | bytes 1048592 | tf_op jit(solution)/shard_map/reduce_scatter | solution.py:216
  463.2 44.1 %reduce-scatter.23.cloned.1.call-done = bf16[2,128,1024]{2,1,0:T(8,128)(2,1)} async-done(((bf16[8,128,1024]{2,1,0:T(8,128)(2,1)}), bf16[2,128,1024]{2,1,0:T(8,128)(2,1)}) %reduce-scatter.23.cloned.1.call-update) | async-done | bytes 524304 | tf_op jit(solution)/shard_map/reduce_scatter | solution.py:208
  512.9 45.0 %all-gather.30.cloned.1.call-done = bf16[8,128,1024]{2,1,0:T(8,128)(2,1)} async-done(((bf16[2,128,1024]{2,1,0:T(8,128)(2,1)}), bf16[8,128,1024]{2,1,0:T(8,128)(2,1)}) %all-gather.30.cloned.1.call-update) | async-done | bytes 2097168 | tf_op jit(solution)/shard_map/all_gather | solution.py:169
  564.0 13.3 %collective-permute-done = bf16[2,128,1024]{2,1,0:T(8,128)(2,1)S(1)} collective-permute-done((bf16[2,128,1024]{2,1,0:T(8,128)(2,1)S(1)}, bf16[2,128,1024]{2,1,0:T(8,128)(2,1)S(1)}, u32[]{:S(2)}, u32[]{:S(2)}) %collective-permute-start) | collective-permute-done | bytes 524320 | tf_op jit(solution)/shard_map/ppermute | solution.py:14
  578.8 46.1 %collective-permute-done.1 = bf16[4,128,1024]{2,1,0:T(8,128)(2,1)} collective-permute-done((bf16[4,128,1024]{2,1,0:T(8,128)(2,1)S(1)}, bf16[4,128,1024]{2,1,0:T(8,128)(2,1)}, u32[]{:S(2)}, u32[]{:S(2)}) %collective-permute-start.1) | collective-permute-done | bytes 1048608 | tf_op jit(solution)/shard_map/ppermute | solution.py:14
  630.2 11.5 copy.100
  641.7 8.5 copy.104
  650.3 21.9 %while.41 = (s32[]{:T(128)}, f32[2,4,4,128]{3,2,1,0:T(4,128)S(1)}, bf16[2,4,128,4,64]{2,4,3,1,0:T(8,128)(2,1)S(1)}, s32[2,4]{1,0:T(2,128)S(1)}, bf16[2,4,128,4,6...) while((s32[]{:T(128)}, f32[2,4,4,128]{3,2,1,0:T(4,128)S(1)}, ...), condition=%wide.region_18.19_spmd.clone.clone, body=%wide.region_15.18_spmd.clone.clone.sunk | while | flops 567674880 | bytes 50406604 | solution.py:179
  673.2 34.7 %while.42 = (s32[]{:T(128)}, bf16[2,4,128,4,64]{2,4,3,1,0:T(8,128)(2,1)}, bf16[2,4,1024,2,4,64]{2,5,4,3,1,0:T(8,128)(2,1)}, bf16[2,4,1024,2,4,64]{2,5,4,1,3,0:T(...) while((s32[]{:T(128)}, ...), condition=%wide.region_21.22_spmd.clone.clone, body=%wide.region_19.21_spmd.clone.clone.sunk | while | flops 1368918016 | bytes 161269104 | solution.py:267
  707.9 11.5 copy.107
  720.9 5.9 bitcast_convert_fusion
  729.8 6.8 bitcast_convert_fusion.1
  743.5 46.9 %reduce-scatter.27.cloned.1.call-done = bf16[8,128,512]{2,1,0:T(8,128)(2,1)} async-done(((bf16[8,1024,512]{2,1,0:T(8,128)(2,1)}), bf16[8,128,512]{2,1,0:T(8,128)(2,1)}) %reduce-scatter.27.cloned.1.call-update) | async-done | bytes 1048592 | tf_op jit(solution)/shard_map/reduce_scatter | solution.py:277
  804.0 23.6 %reduce-scatter.41.cloned.1.call-done = bf16[32,4]{1,0:T(8,128)(2,1)} async-done(((bf16[256,4]{1,0:T(8,128)(2,1)}), bf16[32,4]{1,0:T(8,128)(2,1)}) %reduce-scatter.41.cloned.1.call-update) | async-done | bytes 272
  828.9 42.9 %reduce-scatter.43.cloned.1.call-done = bf16[128,1024]{1,0:T(8,128)(2,1)} async-done(((bf16[1024,1024]{1,0:T(8,128)(2,1)}), bf16[128,1024]{1,0:T(8,128)(2,1)}) %reduce-scatter.43.cloned.1.call-update) | async-done | bytes 262160
  873.8 42.3 %reduce-scatter.37.cloned.1.call-done = bf16[128,1024]{1,0:T(8,128)(2,1)} async-done(((bf16[1024,1024]{1,0:T(8,128)(2,1)}), bf16[128,1024]{1,0:T(8,128)(2,1)}) %reduce-scatter.37.cloned.1.call-update) | async-done | bytes 262160 | tf_op jit(solution)/shard_map/reduce_scatter | solution.py:336
  918.1 35.2 %reduce-scatter.39.cloned.1.call-done = bf16[128,256]{1,0:T(8,128)(2,1)} async-done(((bf16[1024,256]{1,0:T(8,128)(2,1)}), bf16[128,256]{1,0:T(8,128)(2,1)}) %reduce-scatter.39.cloned.1.call-update) | async-done | bytes 65552
  954.8 35.5 %reduce-scatter.31.cloned.1.call-done = bf16[128,256]{1,0:T(8,128)(2,1)} async-done(((bf16[1024,256]{1,0:T(8,128)(2,1)}), bf16[128,256]{1,0:T(8,128)(2,1)}) %reduce-scatter.31.cloned.1.call-update) | async-done | bytes 65552 | tf_op jit(solution)/shard_map/reduce_scatter | solution.py:318
  993.1 12.1 %all-reduce.3 = (bf16[4,64]{1,0:T(4,128)(2,1)S(1)}, bf16[4,64]{1,0:T(4,128)(2,1)S(1)}) all-reduce(bf16[4,64]{1,0:T(4,128)(2,1)S(1)} %reduce_sum.251, bf16[4,64]{1,0:T(4,128)(2,1)S(1)} %convert_element_type.288), channel_id=10, replica_groups=mesh['wide'=8,'tp'=4] {'wide'}, use_global_device_ids=true, to_apply=%region_34.35.clone | all-reduce | flops 512 | bytes 2048
  1005.9 21.5 %reduce-scatter.35.cloned.1.call-done = bf16[128,256]{1,0:T(8,128)(2,1)} async-done(((bf16[1024,256]{1,0:T(8,128)(2,1)}), bf16[128,256]{1,0:T(8,128)(2,1)}) %reduce-scatter.35.cloned.1.call-update) | async-done | bytes 65552 | tf_op jit(solution)/shard_map/reduce_scatter | solution.py:324
  1028.9 36.3 %reduce-scatter.33.cloned.1.call-done = bf16[128,256]{1,0:T(8,128)(2,1)} async-done(((bf16[1024,256]{1,0:T(8,128)(2,1)}), bf16[128,256]{1,0:T(8,128)(2,1)}) %reduce-scatter.33.cloned.1.call-update) | async-done | bytes 65552 | tf_op jit(solution)/shard_map/reduce_scatter | solution.py:321
  1066.7 44.3 %reduce-scatter.29.cloned.1.call-done = bf16[2,128,1024]{2,1,0:T(8,128)(2,1)} async-done(((bf16[8,128,1024]{2,1,0:T(8,128)(2,1)}), bf16[2,128,1024]{2,1,0:T(8,128)(2,1)}) %reduce-scatter.29.cloned.1.call-update) | async-done | bytes 524304 | tf_op jit(solution)/shard_map/reduce_scatter | solution.py:295
  1116.5 39.7 %all-reduce.2 = (f32[1024]{0:T(1024)S(1)}, f32[1024]{0:T(1024)S(1)}, f32[1024]{0:T(1024)S(1)}, f32[1024]{0:T(1024)S(1)}, f32[1024]{0:T(1024)S(1)}, /*index=5*/f32[1024]{0:T(1024)S(1)}) all-reduce(f32[1024]{0:T(1024)S(1)} %get-tuple-element.442, f32[1024]{0:T(1024)S(1)} %get-tuple-element.447, ...), channel_id=1, replica_groups=mesh['wide'=8,'tp'=4] {'wide','tp'}, use_global_device_ids=true, to_apply=%region_27.28 | all-reduce | flops 6144 | bytes 49152 | tf_op jit(solution)/shard_map/psum | solution.py:348
  (353 shorter events, 174.9 us)
Async XLA Ops:
  7.2 69.9 %all-gather.18.cloned.1.call-start = ((), (), s32[]{:S(2)}) async-start(), calls=%async_computation.12 | async-start | bytes 2621440 | tf_op jit(solution)/shard_map/all_gather | solution.py:169
  20.2 491.6 %copy-start.28 = (f32[8,1,128]{2,1,0:T(1,128)}, f32[8,1,128]{2,1,0:T(1,128)S(1)}, u32[]{:S(2)}) copy-start(f32[8,1,128]{2,1,0:T(1,128)S(1)} %convert_element_type.303) | copy-start | bytes 12292
  30.9 107.2 %all-gather.20.cloned.1.call-start = ((), (), s32[]{:S(2)}) async-start(), calls=%async_computation.13 | async-start | bytes 9437184 | tf_op jit(solution)/shard_map/all_gather | solution.py:178
  58.1 499.7 %copy-start.14 = (bf16[1024,256]{1,0:T(8,128)(2,1)}, bf16[1024,256]{1,0:T(8,128)(2,1)S(1)}, u32[]{:S(2)}) copy-start(bf16[1024,256]{1,0:T(8,128)(2,1)S(1)} %all_gather.67) | copy-start | bytes 1572868
  82.9 134.7 %reduce-scatter.21.cloned.1.call-start = ((), (), s32[]{:S(2)}) async-start(), calls=%async_computation.14 | async-start | bytes 2621440 | tf_op jit(solution)/shard_map/reduce_scatter | solution.py:193
  114.2 57.5 %copy-start.22 = (bf16[256,1024]{1,0:T(8,128)(2,1)}, bf16[256,1024]{1,0:T(8,128)(2,1)S(1)}, u32[]{:S(2)}) copy-start(bf16[256,1024]{1,0:T(8,128)(2,1)S(1)} %all_gather.72) | copy-start | bytes 1572868
  171.7 50.9 %copy-start.8 = (bf16[2,128,1024]{2,1,0:T(8,128)(2,1)S(1)}, bf16[2,128,1024]{2,1,0:T(8,128)(2,1)}, u32[]{:S(2)}) copy-start(bf16[2,128,1024]{2,1,0:T(8,128)(2,1)} %param.41) | copy-start | bytes 1572868
  173.7 50.7 %copy-start.48 = (bf16[4,32]{1,0:T(4,128)(2,1)S(1)}, bf16[4,32]{1,0:T(4,128)(2,1)}, u32[]{:S(2)}) copy-start(bf16[4,32]{1,0:T(4,128)(2,1)} %param.38) | copy-start | bytes 772
  173.8 72.5 %all-gather.24.cloned.1.call-start = ((), (), s32[]{:S(2)}) async-start(), calls=%async_computation.16 | async-start | bytes 2359296 | tf_op jit(solution)/shard_map/all_gather | solution.py:125
  174.3 119.6 %all-gather.22.cloned.1.call-start = ((), (), s32[]{:S(2)}) async-start(), calls=%async_computation.15 | async-start | bytes 2621440 | tf_op jit(solution)/shard_map/all_gather | solution.py:202
  222.4 118.1 %all-gather.28.cloned.1.call-start = ((), (), s32[]{:S(2)}) async-start(), calls=%async_computation.19 | async-start | bytes 2621440 | tf_op jit(solution)/shard_map/all_gather | solution.py:203
  222.6 287.5 %copy-start.34 = (f32[2,128]{1,0:T(2,128)}, f32[2,128]{1,0:T(2,128)S(1)}, u32[]{:S(2)}) copy-start(f32[2,128]{1,0:T(2,128)S(1)} %compare_convert_fusion) | copy-start | bytes 3076
  223.6 145.7 %all-gather.26.cloned.1.call-start = ((), (), s32[]{:S(2)}) async-start(), calls=%async_computation.17 | async-start | bytes 2359296 | tf_op jit(solution)/shard_map/all_gather | solution.py:127
  224.3 236.5 %reduce-scatter.25.cloned.1.call-start = ((), (), s32[]{:S(2)}) async-start(), calls=%async_computation.20 | async-start | bytes 5242880 | tf_op jit(solution)/shard_map/reduce_scatter | solution.py:216
  233.6 150.4 %copy-start.44 = (f32[1,2,4,128]{3,1,2,0:T(2,128)}, f32[1,2,4,128]{3,1,2,0:T(2,128)S(1)}, u32[]{:S(2)}) copy-start(f32[1,2,4,128]{3,1,2,0:T(2,128)S(1)} %copy.151) | copy-start | bytes 12292
  383.9 76.9 %copy-start.4 = (bf16[2,128,1024]{2,1,0:T(8,128)(2,1)S(1)}, bf16[2,128,1024]{2,1,0:T(8,128)(2,1)}, u32[]{:S(2)}) copy-start(bf16[2,128,1024]{2,1,0:T(8,128)(2,1)} %reduce-scatter.21.cloned.1.call-done) | copy-start | bytes 1572868
  383.9 123.4 %reduce-scatter.23.cloned.1.call-start = ((), (), s32[]{:S(2)}) async-start(), calls=%async_computation.18 | async-start | bytes 2621440 | tf_op jit(solution)/shard_map/reduce_scatter | solution.py:208
  391.1 166.8 %all-gather.30.cloned.1.call-start = ((), (), s32[]{:S(2)}) async-start(), calls=%async_computation.21 | async-start | bytes 2621440 | tf_op jit(solution)/shard_map/all_gather | solution.py:169
  391.3 120.5 %copy-start = (f32[2,128,1024]{2,1,0:T(8,128)}, f32[2,128,1024]{2,1,0:T(8,128)S(1)}, u32[]{:S(2)}) copy-start(f32[2,128,1024]{2,1,0:T(8,128)S(1)} %convert_element_type.237) | copy-start | bytes 3145732
  511.4 51.1 %copy-start.32 = (f32[2,128]{1,0:T(2,128)}, f32[2,128]{1,0:T(2,128)S(1)}, u32[]{:S(2)}) copy-start(f32[2,128]{1,0:T(2,128)S(1)} %broadcast_multiply_fusion.3) | copy-start | bytes 3076
  511.7 50.8 %copy-start.42 = (f32[2,128]{1,0:T(2,128)}, f32[2,128]{1,0:T(2,128)S(1)}, u32[]{:S(2)}) copy-start(f32[2,128]{1,0:T(2,128)S(1)} %multiply_reduce_fusion.2) | copy-start | bytes 3076
  511.8 50.8 %copy-start.36 = (f32[2,128]{1,0:T(2,128)}, f32[2,128]{1,0:T(2,128)S(1)}, u32[]{:S(2)}) copy-start(f32[2,128]{1,0:T(2,128)S(1)} %fusion.125) | copy-start | bytes 3076
  512.8 117.4 %all-gather.32.cloned.1.call-start = ((), (), s32[]{:S(2)}) async-start(), calls=%async_computation.22 | async-start | bytes 9437184 | tf_op jit(solution)/shard_map/all_gather | solution.py:178
  560.2 64.7 %copy-start.23 = (bf16[256,1024]{1,0:T(8,128)(2,1)S(1)}, bf16[256,1024]{1,0:T(8,128)(2,1)}, u32[]{:S(2)}) copy-start(bf16[256,1024]{1,0:T(8,128)(2,1)} %copy-done.22) | copy-start | bytes 1572868
  563.7 226.7 %reduce-scatter.27.cloned.1.call-start = ((), (), s32[]{:S(2)}) async-start(), calls=%async_computation.23 | async-start | bytes 9437184 | tf_op jit(solution)/shard_map/reduce_scatter | solution.py:277
  563.7 13.6 %collective-permute-start = (bf16[2,128,1024]{2,1,0:T(8,128)(2,1)S(1)}, bf16[2,128,1024]{2,1,0:T(8,128)(2,1)S(1)}, u32[]{:S(2)}, u32[]{:S(2)}) collective-permute-start(bf16[2,128,1024]{2,1,0:T(8,128)(2,1)S(1)} %fusion.123), channel_id=1, source_target_pairs={{0,1},{1,0},{2,3},{3,2},{4,5},{5,4},{6,7},{7,6},{8,9},{9,8},{10,11... | collective-permute-start | bytes 1572872 | tf_op jit(solution)/shard_map/ppermute | solution.py:14
  577.5 49.8 %copy-start.24 = (bf16[4,128,1024]{2,1,0:T(8,128)(2,1)}, bf16[4,128,1024]{2,1,0:T(8,128)(2,1)S(1)}, u32[]{:S(2)}) copy-start(bf16[4,128,1024]{2,1,0:T(8,128)(2,1)S(1)} %maximum_select_fusion.1) | copy-start | bytes 3145732
  577.5 47.4 %collective-permute-start.1 = (bf16[4,128,1024]{2,1,0:T(8,128)(2,1)S(1)}, bf16[4,128,1024]{2,1,0:T(8,128)(2,1)}, u32[]{:S(2)}, u32[]{:S(2)}) collective-permute-start(bf16[4,128,1024]{2,1,0:T(8,128)(2,1)S(1)} %maximum_select_fusion.1), channel_id=1, source_target_pairs={{0,2},{1,3},{2,0},{3,1},{4,6},{5,7},{6,4},{7,5},{8,10},{9,11},{10,... | collective-permute-start | bytes 3145736 | tf_op jit(solution)/shard_map/ppermute | solution.py:14
  719.4 108.1 %reduce-scatter.41.cloned.1.call-start = ((), (), s32[]{:S(2)}) async-start(), calls=%async_computation.30 | async-start | bytes 73728
  720.8 151.0 %reduce-scatter.43.cloned.1.call-start = ((), (), s32[]{:S(2)}) async-start(), calls=%async_computation.31 | async-start | bytes 2359296
  729.8 186.3 %reduce-scatter.37.cloned.1.call-start = ((), (), s32[]{:S(2)}) async-start(), calls=%async_computation.28 | async-start | bytes 2359296 | tf_op jit(solution)/shard_map/reduce_scatter | solution.py:336
  736.6 216.6 %reduce-scatter.39.cloned.1.call-start = ((), (), s32[]{:S(2)}) async-start(), calls=%async_computation.29 | async-start | bytes 589824
  740.2 250.1 %reduce-scatter.31.cloned.1.call-start = ((), (), s32[]{:S(2)}) async-start(), calls=%async_computation.25 | async-start | bytes 589824 | tf_op jit(solution)/shard_map/reduce_scatter | solution.py:318
  743.4 50.3 %copy-start.21 = (bf16[1024,256]{1,0:T(8,128)(2,1)S(1)}, bf16[1024,256]{1,0:T(8,128)(2,1)}, u32[]{:S(2)}) copy-start(bf16[1024,256]{1,0:T(8,128)(2,1)} %copy-done.19) | copy-start | bytes 1572868
  743.5 283.9 %reduce-scatter.35.cloned.1.call-start = ((), (), s32[]{:S(2)}) async-start(), calls=%async_computation.27 | async-start | bytes 589824 | tf_op jit(solution)/shard_map/reduce_scatter | solution.py:324
  793.7 271.5 %reduce-scatter.33.cloned.1.call-start = ((), (), s32[]{:S(2)}) async-start(), calls=%async_computation.26 | async-start | bytes 589824 | tf_op jit(solution)/shard_map/reduce_scatter | solution.py:321
  798.1 312.9 %reduce-scatter.29.cloned.1.call-start = ((), (), s32[]{:S(2)}) async-start(), calls=%async_computation.24 | async-start | bytes 2621440 | tf_op jit(solution)/shard_map/reduce_scatter | solution.py:295
  802.5 308.5 %copy-start.1 = (f32[2,128,1024]{2,1,0:T(8,128)S(1)}, f32[2,128,1024]{2,1,0:T(8,128)}, u32[]{:S(2)}) copy-start(f32[2,128,1024]{2,1,0:T(8,128)} %copy-done) | copy-start | bytes 3145732
  802.5 308.5 %copy-start.29 = (f32[8,1,128]{2,1,0:T(1,128)S(1)}, f32[8,1,128]{2,1,0:T(1,128)}, u32[]{:S(2)}) copy-start(f32[8,1,128]{2,1,0:T(1,128)} %copy-done.28) | copy-start | bytes 12292
  802.5 308.5 %copy-start.33 = (f32[2,128]{1,0:T(2,128)S(1)}, f32[2,128]{1,0:T(2,128)}, u32[]{:S(2)}) copy-start(f32[2,128]{1,0:T(2,128)} %copy-done.32) | copy-start | bytes 3076
  802.5 309.9 %copy-start.43 = (f32[2,128]{1,0:T(2,128)S(1)}, f32[2,128]{1,0:T(2,128)}, u32[]{:S(2)}) copy-start(f32[2,128]{1,0:T(2,128)} %copy-done.42) | copy-start | bytes 3076
  802.5 309.9 %copy-start.37 = (f32[2,128]{1,0:T(2,128)S(1)}, f32[2,128]{1,0:T(2,128)}, u32[]{:S(2)}) copy-start(f32[2,128]{1,0:T(2,128)} %copy-done.36) | copy-start | bytes 3076
  802.5 311.5 %copy-start.6 = (f32[2,128,1024]{2,1,0:T(8,128)S(1)}, f32[2,128,1024]{2,1,0:T(8,128)}, u32[]{:S(2)}) copy-start(f32[2,128,1024]{2,1,0:T(8,128)} %copy-done.5) | copy-start | bytes 3145732
  802.5 311.5 %copy-start.9 = (bf16[2,128,1024]{2,1,0:T(8,128)(2,1)S(1)}, bf16[2,128,1024]{2,1,0:T(8,128)(2,1)}, u32[]{:S(2)}) copy-start(bf16[2,128,1024]{2,1,0:T(8,128)(2,1)} %param.41) | copy-start | bytes 1572868
  802.5 311.5 %copy-start.35 = (f32[2,128]{1,0:T(2,128)S(1)}, f32[2,128]{1,0:T(2,128)}, u32[]{:S(2)}) copy-start(f32[2,128]{1,0:T(2,128)} %copy-done.34) | copy-start | bytes 3076
  802.5 311.5 %copy-start.41 = (f32[2,128]{1,0:T(2,128)S(1)}, f32[2,128]{1,0:T(2,128)}, u32[]{:S(2)}) copy-start(f32[2,128]{1,0:T(2,128)} %copy-done.40) | copy-start | bytes 3076
  918.0 198.5 %copy-start.38 = (f32[1024]{0:T(1024)S(1)}, f32[1024]{0:T(1024)}, u32[]{:S(2)}) copy-start(f32[1024]{0:T(1024)} %get-tuple-element.440) | copy-start | bytes 12292
  918.0 198.5 %copy-start.39 = (f32[1024]{0:T(1024)S(1)}, f32[1024]{0:T(1024)}, u32[]{:S(2)}) copy-start(f32[1024]{0:T(1024)} %get-tuple-element.444) | copy-start | bytes 12292
  (39 other events, 344.9 us)
Sparse Core Ops, SparseCore 0:
  31.1 45.9 all-gather.17
  83.0 55.0 all-gather.19
  173.9 43.6 reduce-scatter.20
  219.3 26.9 all-gather.23
  248.3 45.6 all-gather.21
  296.0 44.4 all-gather.27
  342.3 26.8 all-gather.25
  384.0 76.7 reduce-scatter.24
  463.2 44.0 reduce-scatter.22
  513.0 44.8 all-gather.29
  563.8 53.0 all-gather.31
  719.5 70.8 reduce-scatter.26
  794.0 33.5 reduce-scatter.40
  830.7 41.0 reduce-scatter.42
  874.9 41.1 reduce-scatter.36
  919.0 34.1 reduce-scatter.38
  956.1 34.1 reduce-scatter.30
  993.2 34.1 reduce-scatter.34
  1031.1 34.1 reduce-scatter.32
  1067.4 43.5 reduce-scatter.28
